TPU v7x, 512 devices: a whole 4x4x16 slice. The times are simulated.
512 devices in a mesh: loop: 32 (over z, y_hi), seg: 16 (over x, y_lo, core).
Axes of the slice: x: 4, y: 4 (y_hi: 2, y_lo: 2; y = y_hi * 2 + y_lo), z: 16, core: 2. Of those that a mesh axis runs over, the one named last changes fastest.
Arguments:
- dosage: bfloat16 [8192, 32768], P('seg', 'loop'), may hold values from -3 to 3
- weight_tiles: bfloat16 [3, 1024, 4096], P(None, None, 'loop'), may hold values from -0.109375 to 0.109375
- first_tile: int32 [4096], P('loop'), may hold values from 0 to 1
- last_tile: int32 [4096], P('loop'), may hold values from 1 to 2
Outputs:
- covariance: float32 [4096, 4096], P('seg', 'loop')
Inputs may be any that keep to these rules, and one draw needn't show every extreme that they name: `first_tile`: a gene's window always covers its home slot 1.
All inputs are finite; a program needn't handle non-finite values.
Results may differ from a plain program's by a relative error of at most 0.0021.
Values may be sent and summed in bfloat16 or wider, within the bound.
A program may use at most 64 MiB of HBM per device.

v0:
```python
import jax
import jax.numpy as jnp
from jax import lax
from jax.sharding import PartitionSpec as P


def shifted(value, axis, steps):
    count = lax.axis_size(axis)
    leading, last = (max(0, -steps), min(count, count - steps))
    return lax.ppermute(value, axis, [(source, source + steps) for source in range(leading, last)])


def shards(dosage, weight_tiles, first_tile, last_tile):
    n_slots = weight_tiles.shape[0]
    side_reach = (n_slots - 1) // 2
    slot_index = jnp.arange(n_slots, dtype=jnp.int32)[:, None]
    covered = (slot_index >= first_tile[None, :]) & (slot_index <= last_tile[None, :])
    masked = jnp.where(covered[:, None, :], weight_tiles, jnp.zeros((), weight_tiles.dtype))
    running = jnp.dot(dosage, masked[side_reach], preferred_element_type=jnp.float32)
    for slot_pos in range(n_slots):
        offset = slot_pos - side_reach
        if offset != 0:
            arrived = shifted(dosage, "loop", -offset)
            running = running + jnp.dot(
                arrived, masked[slot_pos], preferred_element_type=jnp.float32
            )
    projection = running.astype(jnp.bfloat16)
    pair_sums = lax.dot_general(
        lax.all_gather(projection, "loop", axis=1, tiled=True),
        projection,
        (((0,), (0,)), ((), ())),
        preferred_element_type=jnp.float32,
    )
    summed = lax.psum_scatter(pair_sums, "seg", scatter_dimension=0, tiled=True)
    sample_total = dosage.shape[0] * lax.axis_size("seg")
    return summed / sample_total


def solution(mesh):
    return jax.shard_map(
        shards,
        mesh=mesh,
        in_specs=(P("seg", "loop"), P(None, None, "loop"), P("loop"), P("loop")),
        out_specs=P("seg", "loop"),
        check_vma=False,
    )
```

profile of v0, /device:TPU:16, one launch (start us, length us, event | category | flops | bytes accessed | tf_op | source)
XLA Modules:
  0.0 306.9 jit_solution(11395456426967035104)
XLA Ops:
  6.5 0.0 all-gather.2.cloned.1.call-start
  6.5 3.6 %collective-permute-start = (bf16[512,1024]{1,0:T(8,128)(2,1)}, bf16[512,1024]{1,0:T(8,128)(2,1)S(1)}, u32[]{:S(2)}, u32[]{:S(2)}) collective-permute-start(bf16[512,1024]{1,0:T(8,128)(2,1)} %param.4), channel_id=1, source_target_pairs={{0,16},{16,32},{32,48},{48,64},{64,80},{80,96},{96,112},{112,128},... | collective-permute-start | bytes 3145736 | tf_op jit(solution)/shard_map/ppermute | solution.py:10
  10.1 5.4 %collective-permute-start.1 = (bf16[512,1024]{1,0:T(8,128)(2,1)}, bf16[512,1024]{1,0:T(8,128)(2,1)S(1)}, u32[]{:S(2)}, u32[]{:S(2)}) collective-permute-start(bf16[512,1024]{1,0:T(8,128)(2,1)} %param.4), channel_id=1, source_target_pairs={{16,0},{32,16},{48,32},{64,48},{80,64},{96,80},{112,96},{128,112},... | collective-permute-start | bytes 3145736 | tf_op jit(solution)/shard_map/ppermute | solution.py:10
  15.5 0.7 fusion.2
  16.2 1.2 broadcast_select_fusion
  17.4 1.7 fusion.1
  19.1 38.4 %collective-permute-done = bf16[512,1024]{1,0:T(8,128)(2,1)S(1)} collective-permute-done((bf16[512,1024]{1,0:T(8,128)(2,1)}, bf16[512,1024]{1,0:T(8,128)(2,1)S(1)}, u32[]{:S(2)}, u32[]{:S(2)}) %collective-permute-start) | collective-permute-done | bytes 1048608 | tf_op jit(solution)/shard_map/ppermute | solution.py:10
  57.5 0.5 convolution_add_fusion.1
  58.0 0.0 collective-permute-done.1
  58.0 1.1 fusion
  59.2 0.0 all-gather.2.cloned.1.call-update
  59.2 0.0 reduce-scatter.2.cloned.1.call-start
  59.2 165.9 %all-gather.2.cloned.1.call-done = bf16[512,4096]{0,1:T(8,128)(2,1)} async-done(((bf16[512,128]{0,1:T(8,128)(2,1)}), bf16[512,4096]{0,1:T(8,128)(2,1)}) %all-gather.2.cloned.1.call-update) | async-done | bytes 4194320 | tf_op jit(solution)/shard_map/all_gather | solution.py:29
  225.1 4.8 %fusion.3 = f32[4096,128]{1,0:T(8,128)} fusion(bf16[512,4096]{0,1:T(8,128)(2,1)} %all-gather.2.cloned.1.call-done, bf16[128,512]{1,0:T(8,128)(2,1)} %fusion), kind=kOutput, calls=%fused_computation.12 | convolution fusion | flops 536870912 | bytes 6422528 | tf_op jit(solution)/shard_map/dot_general | solution.py:28
  229.9 0.0 reduce-scatter.2.cloned.1.call-update
  229.9 68.5 %reduce-scatter.2.cloned.1.call-done = f32[256,128]{1,0:T(8,128)} async-done(((f32[4096,128]{1,0:T(8,128)}), f32[256,128]{1,0:T(8,128)}) %reduce-scatter.2.cloned.1.call-update) | async-done | bytes 131088 | tf_op jit(solution)/shard_map/reduce_scatter | solution.py:34
  298.4 1.6 broadcast_multiply_fusion
Async XLA Ops:
  6.5 218.6 %all-gather.2.cloned.1.call-start = ((), (), s32[]{:S(2)}) async-start(), calls=%async_computation.1 | async-start | bytes 4325376 | tf_op jit(solution)/shard_map/all_gather | solution.py:29
  6.5 51.0 %collective-permute-start = (bf16[512,1024]{1,0:T(8,128)(2,1)}, bf16[512,1024]{1,0:T(8,128)(2,1)S(1)}, u32[]{:S(2)}, u32[]{:S(2)}) collective-permute-start(bf16[512,1024]{1,0:T(8,128)(2,1)} %param.4), channel_id=1, source_target_pairs={{0,16},{16,32},{32,48},{48,64},{64,80},{80,96},{96,112},{112,128},... | collective-permute-start | bytes 3145736 | tf_op jit(solution)/shard_map/ppermute | solution.py:10
  10.1 47.9 %collective-permute-start.1 = (bf16[512,1024]{1,0:T(8,128)(2,1)}, bf16[512,1024]{1,0:T(8,128)(2,1)S(1)}, u32[]{:S(2)}, u32[]{:S(2)}) collective-permute-start(bf16[512,1024]{1,0:T(8,128)(2,1)} %param.4), channel_id=1, source_target_pairs={{16,0},{32,16},{48,32},{64,48},{80,64},{96,80},{112,96},{128,112},... | collective-permute-start | bytes 3145736 | tf_op jit(solution)/shard_map/ppermute | solution.py:10
  59.2 239.3 %reduce-scatter.2.cloned.1.call-start = ((), (), s32[]{:S(2)}) async-start(), calls=%async_computation.2 | async-start | bytes 2228224 | tf_op jit(solution)/shard_map/reduce_scatter | solution.py:34
Sparse Core Ops, SparseCore 0:
  59.3 165.7 all-gather.1
  230.0 68.3 reduce-scatter.1
where the time goes:
time: 307 us
  waiting for transfers between devices  273 us (89%)
  between operations  13.4 us (4%)
  starting transfers between devices  9.01 us (3%)
  matrix products  8.09 us (3%)
  other arithmetic  3.44 us (1%)
    all_gather x1, waiting for transfers between devices, shards(): lax.all_gather(projection, 'loop', axis=1, tiled=True)  166 us
    reduce_scatter x1, waiting for transfers between devices, shards(): summed = lax.psum_scatter(pair_sums, 'seg', scatter_dimension=0, tiled=True)  68.5 us
    ppermute x2, waiting for transfers between devices, shifted(): lax.ppermute(value, axis, [(source, source + steps) for source in range(l...  38.4 us
    ppermute x2, starting transfers between devices, shifted(): lax.ppermute(value, axis, [(source, source + steps) for source in range(l...  8.97 us
  transfers between devices with their start and end apart: 4, of which 3 were waited for; matrix products, arithmetic and copies ran while one was open for 1% of the time, Pallas kernels for 0%

commit v1 on v0

--- a/solution.py
+++ b/solution.py
@@ -26,7 +26,9 @@
             )
     projection = running.astype(jnp.bfloat16)
     pair_sums = lax.dot_general(
-        lax.all_gather(projection, "loop", axis=1, tiled=True),
+        jnp.concatenate(
+            lax.all_to_all(jnp.stack([projection] * lax.axis_size("loop")), "loop", 0, 0), axis=1
+        ),
         projection,
         (((0,), (0,)), ((), ())),
         preferred_element_type=jnp.float32,

time: 307 us -> 341 us (1.11)
  blocking collectives: 0 us -> 207 us
  waiting for transfers between devices: 273 us -> 102 us
    all_to_all x0 -> x1, blocking collectives: none -> 207 us  [shards(): lax.all_to_all(jnp.stack([projection] * lax.axis_size('loop')), 'loop', 0...]
    all_gather x1 -> x0, waiting for transfers between devices: 166 us -> none  [shards(): lax.all_gather(projection, 'loop', axis=1, tiled=True)]
    reduce_scatter x1, waiting for transfers between devices: 68.5 us -> 63.8 us  [shards(): summed = lax.psum_scatter(pair_sums, 'seg', scatter_dimension=0, tiled=True)]
  transfers between devices with their start and end apart: 4 -> 3, of which waited for: 3 -> 2; matrix products, arithmetic and copies ran while one was open for 1% -> 1% of each run, Pallas kernels for 0% -> 0%
where the time goes in v1:
time: 341 us
  blocking collectives  207 us (61%)
  waiting for transfers between devices  102 us (30%)
  between operations  13.5 us (4%)
  starting transfers between devices  8.97 us (3%)
  matrix products  5.26 us (2%)
  other arithmetic  3.44 us (1%)
    all_to_all x1, blocking collectives, shards(): lax.all_to_all(jnp.stack([projection] * lax.axis_size('loop')), 'loop', 0...  207 us
    reduce_scatter x1, waiting for transfers between devices, shards(): summed = lax.psum_scatter(pair_sums, 'seg', scatter_dimension=0, tiled=True)  63.8 us
    ppermute x2, waiting for transfers between devices, shifted(): lax.ppermute(value, axis, [(source, source + steps) for source in range(l...  38.4 us
    ppermute x2, starting transfers between devices, shifted(): lax.ppermute(value, axis, [(source, source + steps) for source in range(l...  8.97 us
  transfers between devices with their start and end apart: 3, of which 2 were waited for; matrix products, arithmetic and copies ran while one was open for 1% of the time, Pallas kernels for 0%

profile of v1, /device:TPU:16, one launch (start us, length us, event | category | flops | bytes accessed | tf_op | source)
XLA Modules:
  0.0 340.5 jit_solution(2694519213567189763)
XLA Ops:
  6.5 0.0 reduce-scatter.2.cloned.1.call-start
  6.5 3.6 %collective-permute-start = (bf16[512,1024]{1,0:T(8,128)(2,1)}, bf16[512,1024]{1,0:T(8,128)(2,1)S(1)}, u32[]{:S(2)}, u32[]{:S(2)}) collective-permute-start(bf16[512,1024]{1,0:T(8,128)(2,1)} %param.4), channel_id=1, source_target_pairs={{0,16},{16,32},{32,48},{48,64},{64,80},{80,96},{96,112},{112,128},... | collective-permute-start | bytes 3145736 | tf_op jit(solution)/shard_map/ppermute | solution.py:10
  10.1 5.4 %collective-permute-start.1 = (bf16[512,1024]{1,0:T(8,128)(2,1)}, bf16[512,1024]{1,0:T(8,128)(2,1)S(1)}, u32[]{:S(2)}, u32[]{:S(2)}) collective-permute-start(bf16[512,1024]{1,0:T(8,128)(2,1)} %param.4), channel_id=1, source_target_pairs={{16,0},{32,16},{48,32},{64,48},{80,64},{96,80},{112,96},{128,112},... | collective-permute-start | bytes 3145736 | tf_op jit(solution)/shard_map/ppermute | solution.py:10
  15.5 0.7 fusion.2
  16.2 1.2 broadcast_select_fusion
  17.4 1.7 fusion.1
  19.1 38.4 %collective-permute-done = bf16[512,1024]{1,0:T(8,128)(2,1)S(1)} collective-permute-done((bf16[512,1024]{1,0:T(8,128)(2,1)}, bf16[512,1024]{1,0:T(8,128)(2,1)S(1)}, u32[]{:S(2)}, u32[]{:S(2)}) %collective-permute-start) | collective-permute-done | bytes 1048608 | tf_op jit(solution)/shard_map/ppermute | solution.py:10
  57.5 0.5 convolution_add_fusion.1
  58.0 0.0 collective-permute-done.1
  58.0 0.5 fusion
  58.5 0.5 stack.2
  59.0 206.7 %all_to_all.5 = bf16[32,512,128]{1,2,0:T(8,128)(2,1)S(1)} all-to-all(bf16[32,512,128]{1,2,0:T(8,128)(2,1)S(1)} %stack.2), channel_id=1, replica_groups=mesh['loop'=32,'seg'=16] {'loop'}, dimensions={0} | all-to-all | bytes 8388608 | tf_op jit(solution)/shard_map/all_to_all | solution.py:30
  265.7 2.6 fusion.3
  268.2 0.0 reduce-scatter.2.cloned.1.call-update
  268.3 63.8 %reduce-scatter.2.cloned.1.call-done = f32[256,128]{1,0:T(8,128)} async-done(((f32[4096,128]{1,0:T(8,128)}), f32[256,128]{1,0:T(8,128)}) %reduce-scatter.2.cloned.1.call-update) | async-done | bytes 131088 | tf_op jit(solution)/shard_map/reduce_scatter | solution.py:36
  332.1 1.6 broadcast_multiply_fusion
Async XLA Ops:
  6.5 325.6 %reduce-scatter.2.cloned.1.call-start = ((), (), s32[]{:S(2)}) async-start(), calls=%async_computation.2 | async-start | bytes 2228224 | tf_op jit(solution)/shard_map/reduce_scatter | solution.py:36
  6.5 51.0 %collective-permute-start = (bf16[512,1024]{1,0:T(8,128)(2,1)}, bf16[512,1024]{1,0:T(8,128)(2,1)S(1)}, u32[]{:S(2)}, u32[]{:S(2)}) collective-permute-start(bf16[512,1024]{1,0:T(8,128)(2,1)} %param.4), channel_id=1, source_target_pairs={{0,16},{16,32},{32,48},{48,64},{64,80},{80,96},{96,112},{112,128},... | collective-permute-start | bytes 3145736 | tf_op jit(solution)/shard_map/ppermute | solution.py:10
  10.1 47.9 %collective-permute-start.1 = (bf16[512,1024]{1,0:T(8,128)(2,1)}, bf16[512,1024]{1,0:T(8,128)(2,1)S(1)}, u32[]{:S(2)}, u32[]{:S(2)}) collective-permute-start(bf16[512,1024]{1,0:T(8,128)(2,1)} %param.4), channel_id=1, source_target_pairs={{16,0},{32,16},{48,32},{64,48},{80,64},{96,80},{112,96},{128,112},... | collective-permute-start | bytes 3145736 | tf_op jit(solution)/shard_map/ppermute | solution.py:10
Sparse Core Ops, SparseCore 0:
  268.4 63.6 reduce-scatter.1
